TPU v7x, 32 devices: a whole 2x2x4 slice. The times are simulated.
32 devices in a mesh: groups: 2 (over y), seq: 8 (over z, x), chan: 2 (over core).
Axes of the slice: x: 2, y: 2, z: 4, core: 2. Of those that a mesh axis runs over, the one named last changes fastest.
Arguments:
- projected: bfloat16 [3, 2048, 1024], P(None, ('groups', 'seq'), 'chan'), parts along dimension 1, may hold values from -6 to 6
- long_filter: float32 [2048, 1024], P(('groups', 'seq'), 'chan'), parts along dimension 0, may hold values from -6 to 6
- short_kernel: float32 [3, 7, 1024], P(None, None, 'chan'), may hold values from -2 to 2
- skip_gain: float32 [1024], P('chan'), may hold values from 0.25 to 1.5
- cotangent: bfloat16 [2048, 1024], P(('groups', 'seq'), 'chan'), parts along dimension 0, may hold values from -6 to 6
Outputs:
- layer_output: bfloat16 [2048, 1024], P(('groups', 'seq'), 'chan'), parts along dimension 0
- stream_grads: bfloat16 [3, 2048, 1024], P(None, ('groups', 'seq'), 'chan'), parts along dimension 1
- filter_grad: float32 [2048, 1024], P(('groups', 'seq'), 'chan'), parts along dimension 0
- kernel_grad: float32 [6, 7, 1024], P('groups', None, 'chan'), parts along dimension 0
- skip_grad: float32 [2048], P(('groups', 'chan')), parts along dimension 0
There are 2 independent parts, one for each index of `groups`. A program takes and returns all parts, laid end to end along the dimension named above; an argument that names none is the same for every part. Nothing has to cross between parts.
All inputs are finite; a program needn't handle non-finite values.
Results may differ from a plain program's by a relative error of at most 0.001.
Values may be sent and summed in bfloat16 or wider, within the bound.
A program may use at most 64 MiB of HBM per device.

v0:
```python
import math
import jax
import jax.numpy as jnp
from jax import lax
from jax.sharding import PartitionSpec as P

HIGHEST = lax.Precision.HIGHEST


def with_halo(block, sides, width):
    for axis, dim in sides:
        count = lax.axis_size(axis)
        forward = [(i, i + 1) for i in range(count - 1)]
        forward.append((count - 1, 0))
        backward = [(target, source) for source, target in forward]
        low = lax.ppermute(
            lax.slice_in_dim(block, block.shape[dim] - width, None, axis=dim), axis, forward
        )
        high = lax.ppermute(lax.slice_in_dim(block, 0, width, axis=dim), axis, backward)
        block = jnp.concatenate([low, block, high], axis=dim)
    return block


def dft_tables(extent):
    indices = jnp.arange(extent, dtype=jnp.int32)
    angles = (indices[:, None] * indices[None, :] % extent).astype(jnp.float32) * (
        2.0 * math.pi / extent
    )
    return (jnp.cos(angles), jnp.sin(angles))


def apply_along(matrix, signal, axis_dim):
    letters = "wxyz"
    target = letters[:axis_dim] + "k" + letters[axis_dim + 1 :]
    return jnp.einsum(
        "k" + letters[axis_dim] + "," + letters + "->" + target, matrix, signal, precision=HIGHEST
    )


def forward_section(real_part, imaginary, axis_dim):
    cosine, sine_table = dft_tables(real_part.shape[axis_dim])
    out_real = apply_along(cosine, real_part, axis_dim)
    out_imag = -apply_along(sine_table, real_part, axis_dim)
    if imaginary is not None:
        out_real = out_real + apply_along(sine_table, imaginary, axis_dim)
        out_imag = out_imag + apply_along(cosine, imaginary, axis_dim)
    return (out_real, out_imag)


def inverse_section(real_part, imaginary, axis_dim, keep_imag):
    cosine, sine_table = dft_tables(real_part.shape[axis_dim])
    out_real = apply_along(cosine, real_part, axis_dim) - apply_along(
        sine_table, imaginary, axis_dim
    )
    if keep_imag:
        return (
            out_real,
            apply_along(sine_table, real_part, axis_dim) + apply_along(cosine, imaginary, axis_dim),
        )
    return (out_real, None)


def twist(real_part, imaginary, angles, sign_factor):
    cosine = jnp.cos(angles)
    sine_table = jnp.sin(angles)
    return (
        real_part * cosine + sign_factor * imaginary * sine_table,
        imaginary * cosine - sign_factor * real_part * sine_table,
    )


def twiddle(low_index, high_index, extent):
    return (low_index * high_index % extent).astype(jnp.float32) * (2.0 * math.pi / extent)


def block_angles(devices, portion, extent):
    low_index = jnp.arange(devices, dtype=jnp.int32)[None, :, None, None]
    high_index = (lax.axis_index("seq") * portion + jnp.arange(portion, dtype=jnp.int32))[
        None, None, :, None
    ]
    return twiddle(low_index, high_index, extent)


def sequence_forward(signals, extent):
    devices = lax.axis_size("seq")
    portion = signals.shape[1] // devices
    columns = lax.all_to_all(signals[:, None], "seq", split_axis=2, concat_axis=1, tiled=True)
    real_part, imaginary = forward_section(columns, None, 1)
    real_part, imaginary = twist(real_part, imaginary, block_angles(devices, portion, extent), 1.0)
    spread = (
        lax.all_to_all(real_part, "seq", split_axis=1, concat_axis=2, tiled=True),
        lax.all_to_all(imaginary, "seq", split_axis=1, concat_axis=2, tiled=True),
    )
    return forward_section(spread[0], spread[1], 2)


def sequence_inverse(real_part, imaginary, extent):
    devices = lax.axis_size("seq")
    portion = real_part.shape[2] // devices
    real_part, imaginary = inverse_section(real_part, imaginary, 2, True)
    gathered = (
        lax.all_to_all(real_part, "seq", split_axis=2, concat_axis=1, tiled=True),
        lax.all_to_all(imaginary, "seq", split_axis=2, concat_axis=1, tiled=True),
    )
    real_part, imaginary = twist(
        gathered[0], gathered[1], block_angles(devices, portion, extent), -1.0
    )
    pieces = inverse_section(real_part, imaginary, 1, False)[0] * (1.0 / extent)
    blocks = lax.all_to_all(pieces, "seq", split_axis=1, concat_axis=2, tiled=True)
    return blocks[:, 0]


def body(projected, long_filter, short_kernel, skip_gain, cotangent):
    rows_here = projected.shape[1]
    extent = rows_here * lax.axis_size("seq")
    factor = 1.0 / math.sqrt(extent)
    kernel_span = short_kernel.shape[1]
    margin = kernel_span // 2
    padded = with_halo(projected, (("seq", 1),), margin)
    shorts = jnp.zeros(projected.shape, jnp.float32)
    for offset in range(kernel_span):
        shorts = shorts + short_kernel[:, offset][:, None, :] * padded[
            :, offset : offset + rows_here
        ].astype(jnp.float32)
    gated_signal = shorts[1] * shorts[2]
    transform, restore = (sequence_forward, sequence_inverse)
    upstream = cotangent.astype(jnp.float32)
    grad_response = upstream * shorts[0]
    spec_real, spec_imag = transform(jnp.stack([gated_signal, long_filter]), extent)
    gated_real, gated_imag = (spec_real[0], spec_imag[0])
    filter_real, filter_imag = (spec_real[1] * factor, spec_imag[1] * factor)
    product_real = filter_real * gated_real - filter_imag * gated_imag
    product_imag = filter_real * gated_imag + filter_imag * gated_real
    convolved = restore(product_real[None], product_imag[None], extent)[0]
    upstream_real, upstream_imag = transform(grad_response[None], extent)
    upstream_real, upstream_imag = (upstream_real[0], upstream_imag[0])
    back_real = jnp.stack(
        [
            filter_real * upstream_real + filter_imag * upstream_imag,
            gated_real * upstream_real + gated_imag * upstream_imag,
        ]
    )
    back_imag = jnp.stack(
        [
            filter_real * upstream_imag - filter_imag * upstream_real,
            gated_real * upstream_imag - gated_imag * upstream_real,
        ]
    )
    restored = restore(back_real, back_imag, extent)
    grad_gated = restored[0] + skip_gain * grad_response
    filter_grad = restored[1] * factor
    response = convolved + skip_gain * gated_signal
    layer_output = (response * shorts[0]).astype(jnp.bfloat16)
    grad_shorts = jnp.stack([upstream * response, grad_gated * shorts[2], grad_gated * shorts[1]])
    rimmed = with_halo(grad_shorts, (("seq", 1),), margin)
    stream_sum = jnp.zeros(grad_shorts.shape, jnp.float32)
    kernel_terms = []
    for offset in range(kernel_span):
        start_row = 2 * margin - offset
        stream_sum = (
            stream_sum
            + short_kernel[:, offset][:, None, :] * rimmed[:, start_row : start_row + rows_here]
        )
        kernel_terms.append(
            jnp.sum(
                grad_shorts * padded[:, offset : offset + rows_here].astype(jnp.float32), axis=1
            )
        )
    kernel_part = jnp.stack(kernel_terms, axis=1)
    skip_part = jnp.sum(grad_response * gated_signal, axis=0)
    kernel_total, skip_total = lax.psum((kernel_part, skip_part), "seq")
    return (
        layer_output,
        stream_sum.astype(jnp.bfloat16),
        filter_grad,
        kernel_total * factor,
        skip_total * factor,
    )


def solution(mesh):
    placed = (
        P(None, ("groups", "seq"), "chan"),
        P(("groups", "seq"), "chan"),
        P(None, None, "chan"),
        P("chan"),
        P(("groups", "seq"), "chan"),
    )
    return jax.shard_map(
        body,
        mesh=mesh,
        in_specs=placed,
        out_specs=(
            P(("groups", "seq"), "chan"),
            P(None, ("groups", "seq"), "chan"),
            P(("groups", "seq"), "chan"),
            P("groups", None, "chan"),
            P(("groups", "chan")),
        ),
        check_vma=False,
    )
```

profile of v0, /device:TPU:0, one launch (start us, length us, event | category | flops | bytes accessed | tf_op | source)
XLA Modules:
  0.0 248.4 jit_solution(6842409723577557810)
XLA Ops:
  1.4 6.0 %collective-permute-start.1 = (bf16[3,3,512]{2,1,0:T(4,128)(2,1)S(1)}, bf16[3,3,512]{2,1,0:T(4,128)(2,1)S(1)}, u32[]{:S(2)}, u32[]{:S(2)}) collective-permute-start(bf16[3,3,512]{2,1,0:T(4,128)(2,1)S(1)} %get-tuple-element.52), channel_id=1, source_target_pairs={{2,0},{4,2},{6,4},{8,6},{10,8},{12,10},{14,12},{0,14},{3,1},{5,3},... | collective-permute-start | bytes 27656 | tf_op jit(solution)/shard_map/ppermute | solution.py:19
  8.9 5.0 %collective-permute-done = bf16[3,3,512]{2,1,0:T(4,128)(2,1)S(1)} collective-permute-done((bf16[3,3,512]{2,1,0:T(4,128)(2,1)S(1)}, bf16[3,3,512]{2,1,0:T(4,128)(2,1)S(1)}, u32[]{:S(2)}, u32[]{:S(2)}) %collective-permute-start) | collective-permute-done | bytes 9248 | tf_op jit(solution)/shard_map/ppermute | solution.py:16
  21.4 6.0 %all-to-all-done.6 = f32[1,1,128,512]{3,1,0,2:T(1,128)S(1)} async-done(((f32[1,1,128,512]{3,1,0,2:T(1,128)}), f32[1,1,128,512]{3,1,0,2:T(1,128)S(1)}, u32[]{:S(2)}, u32[]{:S(2)}) %all-to-all-start.6) | async-done | bytes 262176 | tf_op jit(solution)/shard_map/all_to_all | solution.py:87
  27.3 3.5 %all-to-all-start = ((f32[2,1,128,512]{3,0,1,2:T(2,128)}), f32[2,1,128,512]{3,0,1,2:T(2,128)S(1)}, u32[]{:S(2)}, u32[]{:S(2)}) async-start(f32[2,1,128,512]{3,0,1,2:T(2,128)} %copy.42), calls=%async_computation | async-start | bytes 1048576 | tf_op jit(solution)/shard_map/all_to_all | solution.py:87
  33.0 10.4 %all-to-all-done = f32[2,1,128,512]{3,0,1,2:T(2,128)S(1)} async-done(((f32[2,1,128,512]{3,0,1,2:T(2,128)}), f32[2,1,128,512]{3,0,1,2:T(2,128)S(1)}, u32[]{:S(2)}, u32[]{:S(2)}) %all-to-all-start) | async-done | bytes 524320 | tf_op jit(solution)/shard_map/all_to_all | solution.py:87
  43.4 3.6 %all-to-all-start.7 = ((f32[1,8,16,512]{3,2,0,1:T(8,128)}), f32[1,8,16,512]{3,2,0,1:T(8,128)S(1)}, u32[]{:S(2)}, u32[]{:S(2)}) async-start(f32[1,8,16,512]{3,2,0,1:T(8,128)} %copy.64), calls=%async_computation.7 | async-start | bytes 524288 | tf_op jit(solution)/shard_map/all_to_all | solution.py:91
  48.0 7.3 %all-to-all-done.7 = f32[1,8,16,512]{3,2,0,1:T(8,128)S(1)} async-done(((f32[1,8,16,512]{3,2,0,1:T(8,128)}), f32[1,8,16,512]{3,2,0,1:T(8,128)S(1)}, u32[]{:S(2)}, u32[]{:S(2)}) %all-to-all-start.7) | async-done | bytes 262176 | tf_op jit(solution)/shard_map/all_to_all | solution.py:91
  61.7 5.2 %all-to-all-done.8 = f32[1,8,16,512]{3,2,0,1:T(8,128)S(1)} async-done(((f32[1,8,16,512]{3,2,0,1:T(8,128)}), f32[1,8,16,512]{3,2,0,1:T(8,128)S(1)}, u32[]{:S(2)}, u32[]{:S(2)}) %all-to-all-start.8) | async-done | bytes 262176 | tf_op jit(solution)/shard_map/all_to_all | solution.py:92
  71.5 12.8 %all-to-all-done.2 = f32[2,8,16,512]{3,2,0,1:T(8,128)S(1)} async-done(((f32[2,8,16,512]{3,2,0,1:T(8,128)}), f32[2,8,16,512]{3,2,0,1:T(8,128)S(1)}, u32[]{:S(2)}, u32[]{:S(2)}) %all-to-all-start.2) | async-done | bytes 524320 | tf_op jit(solution)/shard_map/all_to_all | solution.py:92
  84.3 3.7 %all-to-all-start.1 = ((f32[2,8,16,512]{3,2,0,1:T(8,128)}), f32[2,8,16,512]{3,2,0,1:T(8,128)S(1)}, u32[]{:S(2)}, u32[]{:S(2)}) async-start(f32[2,8,16,512]{3,2,0,1:T(8,128)} %copy.46), calls=%async_computation.1 | async-start | bytes 1048576 | tf_op jit(solution)/shard_map/all_to_all | solution.py:91
  92.8 9.4 %all-to-all-done.1 = f32[2,8,16,512]{3,2,0,1:T(8,128)S(1)} async-done(((f32[2,8,16,512]{3,2,0,1:T(8,128)}), f32[2,8,16,512]{3,2,0,1:T(8,128)S(1)}, u32[]{:S(2)}, u32[]{:S(2)}) %all-to-all-start.1) | async-done | bytes 524320 | tf_op jit(solution)/shard_map/all_to_all | solution.py:91
  111.0 4.1 %all-to-all-start.9 = ((f32[2,1,128,512]{3,0,1,2:T(2,128)}), f32[2,1,128,512]{3,0,1,2:T(2,128)}, u32[]{:S(2)}, u32[]{:S(2)}) async-start(f32[2,1,128,512]{3,0,1,2:T(2,128)} %copy.66), calls=%async_computation.9 | async-start | bytes 1048576 | tf_op jit(solution)/shard_map/all_to_all | solution.py:102
  117.8 11.4 %all-to-all-done.9 = f32[2,1,128,512]{3,0,1,2:T(2,128)} async-done(((f32[2,1,128,512]{3,0,1,2:T(2,128)}), f32[2,1,128,512]{3,0,1,2:T(2,128)}, u32[]{:S(2)}, u32[]{:S(2)}) %all-to-all-start.9) | async-done | bytes 524320 | tf_op jit(solution)/shard_map/all_to_all | solution.py:102
  129.2 3.7 %all-to-all-start.10 = ((f32[2,1,128,512]{3,0,1,2:T(2,128)}), f32[2,1,128,512]{3,0,1,2:T(2,128)S(1)}, u32[]{:S(2)}, u32[]{:S(2)}) async-start(f32[2,1,128,512]{3,0,1,2:T(2,128)} %copy.69), calls=%async_computation.10 | async-start | bytes 1048576 | tf_op jit(solution)/shard_map/all_to_all | solution.py:103
  135.0 12.2 %all-to-all-done.10 = f32[2,1,128,512]{3,0,1,2:T(2,128)S(1)} async-done(((f32[2,1,128,512]{3,0,1,2:T(2,128)}), f32[2,1,128,512]{3,0,1,2:T(2,128)S(1)}, u32[]{:S(2)}, u32[]{:S(2)}) %all-to-all-start.10) | async-done | bytes 524320 | tf_op jit(solution)/shard_map/all_to_all | solution.py:103
  147.2 3.6 %all-to-all-start.4 = ((f32[1,1,128,512]{3,1,0,2:T(1,128)}), f32[1,1,128,512]{3,1,0,2:T(1,128)S(1)}, u32[]{:S(2)}, u32[]{:S(2)}) async-start(f32[1,1,128,512]{3,1,0,2:T(1,128)} %copy.56), calls=%async_computation.4 | async-start | bytes 524288 | tf_op jit(solution)/shard_map/all_to_all | solution.py:103
  154.1 5.7 %all-to-all-done.4 = f32[1,1,128,512]{3,1,0,2:T(1,128)S(1)} async-done(((f32[1,1,128,512]{3,1,0,2:T(1,128)}), f32[1,1,128,512]{3,1,0,2:T(1,128)S(1)}, u32[]{:S(2)}, u32[]{:S(2)}) %all-to-all-start.4) | async-done | bytes 262176 | tf_op jit(solution)/shard_map/all_to_all | solution.py:103
  159.8 3.6 %all-to-all-start.3 = ((f32[1,1,128,512]{3,1,0,2:T(1,128)}), f32[1,1,128,512]{3,1,0,2:T(1,128)S(1)}, u32[]{:S(2)}, u32[]{:S(2)}) async-start(f32[1,1,128,512]{3,1,0,2:T(1,128)} %copy.54), calls=%async_computation.3 | async-start | bytes 524288 | tf_op jit(solution)/shard_map/all_to_all | solution.py:102
  166.9 5.1 %all-to-all-done.3 = f32[1,1,128,512]{3,1,0,2:T(1,128)S(1)} async-done(((f32[1,1,128,512]{3,1,0,2:T(1,128)}), f32[1,1,128,512]{3,1,0,2:T(1,128)S(1)}, u32[]{:S(2)}, u32[]{:S(2)}) %all-to-all-start.3) | async-done | bytes 262176 | tf_op jit(solution)/shard_map/all_to_all | solution.py:102
  172.0 3.6 %all-to-all-start.11 = ((f32[2,8,16,512]{3,2,0,1:T(8,128)}), f32[2,8,16,512]{3,2,0,1:T(8,128)S(1)}, u32[]{:S(2)}, u32[]{:S(2)}) async-start(f32[2,8,16,512]{3,2,0,1:T(8,128)} %copy.74), calls=%async_computation.11 | async-start | bytes 1048576 | tf_op jit(solution)/shard_map/all_to_all | solution.py:109
  177.8 11.8 %all-to-all-done.11 = f32[2,8,16,512]{3,2,0,1:T(8,128)S(1)} async-done(((f32[2,8,16,512]{3,2,0,1:T(8,128)}), f32[2,8,16,512]{3,2,0,1:T(8,128)S(1)}, u32[]{:S(2)}, u32[]{:S(2)}) %all-to-all-start.11) | async-done | bytes 524320 | tf_op jit(solution)/shard_map/all_to_all | solution.py:109
  189.6 3.6 %all-to-all-start.5 = ((f32[1,8,16,512]{3,2,0,1:T(8,128)}), f32[1,8,16,512]{3,2,0,1:T(8,128)S(1)}, u32[]{:S(2)}, u32[]{:S(2)}) async-start(f32[1,8,16,512]{3,2,0,1:T(8,128)} %copy.60), calls=%async_computation.5 | async-start | bytes 524288 | tf_op jit(solution)/shard_map/all_to_all | solution.py:109
  193.3 8.6 %all-to-all-done.5 = f32[1,8,16,512]{3,2,0,1:T(8,128)S(1)} async-done(((f32[1,8,16,512]{3,2,0,1:T(8,128)}), f32[1,8,16,512]{3,2,0,1:T(8,128)S(1)}, u32[]{:S(2)}, u32[]{:S(2)}) %all-to-all-start.5) | async-done | bytes 262176 | tf_op jit(solution)/shard_map/all_to_all | solution.py:109
  204.5 35.7 %all-reduce = (f32[3,7,512]{2,0,1:T(4,128)S(1)}, f32[512]{0:T(512)S(1)}) all-reduce(f32[3,7,512]{2,0,1:T(4,128)S(1)} %constant_dynamic-update-slice_fusion.2, f32[512]{0:T(512)S(1)} %get-tuple-element.38), channel_id=1, replica_groups=mesh['groups'=2,'seq'=8,'chan'=2] {'seq'}, use_global_device_ids=true, to_apply=%region_7.8 | all-reduce | flops 11264 | bytes 90112 | tf_op jit(solution)/shard_map/psum | solution.py:171
  (101 shorter events, 61.7 us)
Async XLA Ops:
  0.6 6.8 %copy-start.5 = (f32[3,7,512]{2,1,0:T(8,128)S(1)}, f32[3,7,512]{2,1,0:T(8,128)}, u32[]{:S(2)}) copy-start(f32[3,7,512]{2,1,0:T(8,128)} %param.7) | copy-start | bytes 129028
  1.4 7.4 %collective-permute-start.1 = (bf16[3,3,512]{2,1,0:T(4,128)(2,1)S(1)}, bf16[3,3,512]{2,1,0:T(4,128)(2,1)S(1)}, u32[]{:S(2)}, u32[]{:S(2)}) collective-permute-start(bf16[3,3,512]{2,1,0:T(4,128)(2,1)S(1)} %get-tuple-element.52), channel_id=1, source_target_pairs={{2,0},{4,2},{6,4},{8,6},{10,8},{12,10},{14,12},{0,14},{3,1},{5,3},... | collective-permute-start | bytes 27656 | tf_op jit(solution)/shard_map/ppermute | solution.py:19
  7.5 6.4 %collective-permute-start = (bf16[3,3,512]{2,1,0:T(4,128)(2,1)S(1)}, bf16[3,3,512]{2,1,0:T(4,128)(2,1)S(1)}, u32[]{:S(2)}, u32[]{:S(2)}) collective-permute-start(bf16[3,3,512]{2,1,0:T(4,128)(2,1)S(1)} %get-tuple-element.53), channel_id=1, source_target_pairs={{0,2},{2,4},{4,6},{6,8},{8,10},{10,12},{12,14},{14,0},{1,3},{3,5},... | collective-permute-start | bytes 27656 | tf_op jit(solution)/shard_map/ppermute | solution.py:16
  7.5 6.3 %copy-start = (bf16[3,128,512]{2,1,0:T(8,128)(2,1)S(1)}, bf16[3,128,512]{2,1,0:T(8,128)(2,1)}, u32[]{:S(2)}) copy-start(bf16[3,128,512]{2,1,0:T(8,128)(2,1)} %param.5) | copy-start | bytes 1179652
  13.8 0.9 copy-start.3
  15.8 11.6 %all-to-all-start.6 = ((f32[1,1,128,512]{3,1,0,2:T(1,128)}), f32[1,1,128,512]{3,1,0,2:T(1,128)S(1)}, u32[]{:S(2)}, u32[]{:S(2)}) async-start(f32[1,1,128,512]{3,1,0,2:T(1,128)} %copy.61), calls=%async_computation.6 | async-start | bytes 524288 | tf_op jit(solution)/shard_map/all_to_all | solution.py:87
  19.2 1.0 copy-start.4
  27.3 16.0 %all-to-all-start = ((f32[2,1,128,512]{3,0,1,2:T(2,128)}), f32[2,1,128,512]{3,0,1,2:T(2,128)S(1)}, u32[]{:S(2)}, u32[]{:S(2)}) async-start(f32[2,1,128,512]{3,0,1,2:T(2,128)} %copy.42), calls=%async_computation | async-start | bytes 1048576 | tf_op jit(solution)/shard_map/all_to_all | solution.py:87
  43.4 11.9 %all-to-all-start.7 = ((f32[1,8,16,512]{3,2,0,1:T(8,128)}), f32[1,8,16,512]{3,2,0,1:T(8,128)S(1)}, u32[]{:S(2)}, u32[]{:S(2)}) async-start(f32[1,8,16,512]{3,2,0,1:T(8,128)} %copy.64), calls=%async_computation.7 | async-start | bytes 524288 | tf_op jit(solution)/shard_map/all_to_all | solution.py:91
  55.3 11.6 %all-to-all-start.8 = ((f32[1,8,16,512]{3,2,0,1:T(8,128)}), f32[1,8,16,512]{3,2,0,1:T(8,128)S(1)}, u32[]{:S(2)}, u32[]{:S(2)}) async-start(f32[1,8,16,512]{3,2,0,1:T(8,128)} %copy.65), calls=%async_computation.8 | async-start | bytes 524288 | tf_op jit(solution)/shard_map/all_to_all | solution.py:92
  66.9 17.4 %all-to-all-start.2 = ((f32[2,8,16,512]{3,2,0,1:T(8,128)}), f32[2,8,16,512]{3,2,0,1:T(8,128)S(1)}, u32[]{:S(2)}, u32[]{:S(2)}) async-start(f32[2,8,16,512]{3,2,0,1:T(8,128)} %copy.49), calls=%async_computation.2 | async-start | bytes 1048576 | tf_op jit(solution)/shard_map/all_to_all | solution.py:92
  84.3 17.9 %all-to-all-start.1 = ((f32[2,8,16,512]{3,2,0,1:T(8,128)}), f32[2,8,16,512]{3,2,0,1:T(8,128)S(1)}, u32[]{:S(2)}, u32[]{:S(2)}) async-start(f32[2,8,16,512]{3,2,0,1:T(8,128)} %copy.46), calls=%async_computation.1 | async-start | bytes 1048576 | tf_op jit(solution)/shard_map/all_to_all | solution.py:91
  104.5 1.2 copy-start.1
  104.5 1.2 copy-start.2
  111.0 18.2 %all-to-all-start.9 = ((f32[2,1,128,512]{3,0,1,2:T(2,128)}), f32[2,1,128,512]{3,0,1,2:T(2,128)}, u32[]{:S(2)}, u32[]{:S(2)}) async-start(f32[2,1,128,512]{3,0,1,2:T(2,128)} %copy.66), calls=%async_computation.9 | async-start | bytes 1048576 | tf_op jit(solution)/shard_map/all_to_all | solution.py:102
  129.2 18.0 %all-to-all-start.10 = ((f32[2,1,128,512]{3,0,1,2:T(2,128)}), f32[2,1,128,512]{3,0,1,2:T(2,128)S(1)}, u32[]{:S(2)}, u32[]{:S(2)}) async-start(f32[2,1,128,512]{3,0,1,2:T(2,128)} %copy.69), calls=%async_computation.10 | async-start | bytes 1048576 | tf_op jit(solution)/shard_map/all_to_all | solution.py:103
  147.2 12.6 %all-to-all-start.4 = ((f32[1,1,128,512]{3,1,0,2:T(1,128)}), f32[1,1,128,512]{3,1,0,2:T(1,128)S(1)}, u32[]{:S(2)}, u32[]{:S(2)}) async-start(f32[1,1,128,512]{3,1,0,2:T(1,128)} %copy.56), calls=%async_computation.4 | async-start | bytes 524288 | tf_op jit(solution)/shard_map/all_to_all | solution.py:103
  159.8 12.2 %all-to-all-start.3 = ((f32[1,1,128,512]{3,1,0,2:T(1,128)}), f32[1,1,128,512]{3,1,0,2:T(1,128)S(1)}, u32[]{:S(2)}, u32[]{:S(2)}) async-start(f32[1,1,128,512]{3,1,0,2:T(1,128)} %copy.54), calls=%async_computation.3 | async-start | bytes 524288 | tf_op jit(solution)/shard_map/all_to_all | solution.py:102
  172.0 17.6 %all-to-all-start.11 = ((f32[2,8,16,512]{3,2,0,1:T(8,128)}), f32[2,8,16,512]{3,2,0,1:T(8,128)S(1)}, u32[]{:S(2)}, u32[]{:S(2)}) async-start(f32[2,8,16,512]{3,2,0,1:T(8,128)} %copy.74), calls=%async_computation.11 | async-start | bytes 1048576 | tf_op jit(solution)/shard_map/all_to_all | solution.py:109
  189.6 12.3 %all-to-all-start.5 = ((f32[1,8,16,512]{3,2,0,1:T(8,128)}), f32[1,8,16,512]{3,2,0,1:T(8,128)S(1)}, u32[]{:S(2)}, u32[]{:S(2)}) async-start(f32[1,8,16,512]{3,2,0,1:T(8,128)} %copy.60), calls=%async_computation.5 | async-start | bytes 524288 | tf_op jit(solution)/shard_map/all_to_all | solution.py:109
  193.2 8.7 %copy-start.6 = (f32[512]{0:T(512)S(1)}, f32[512]{0:T(512)}, u32[]{:S(2)}) copy-start(f32[512]{0:T(512)} %param.8) | copy-start | bytes 6148
  240.3 4.0 %collective-permute-start.2 = (f32[3,3,512]{2,1,0:T(4,128)S(1)}, f32[3,3,512]{2,1,0:T(4,128)S(1)}, u32[]{:S(2)}, u32[]{:S(2)}) collective-permute-start(f32[3,3,512]{2,1,0:T(4,128)S(1)} %get-tuple-element.46), channel_id=1, source_target_pairs={{2,0},{4,2},{6,4},{8,6},{10,8},{12,10},{14,12},{0,14},{3,1},{5,3},... | collective-permute-start | bytes 55304 | tf_op jit(solution)/shard_map/ppermute | solution.py:19
  240.4 6.6 %collective-permute-start.3 = (f32[3,3,512]{2,1,0:T(4,128)S(1)}, f32[3,3,512]{2,1,0:T(4,128)S(1)}, u32[]{:S(2)}, u32[]{:S(2)}) collective-permute-start(f32[3,3,512]{2,1,0:T(4,128)S(1)} %get-tuple-element.47), channel_id=1, source_target_pairs={{0,2},{2,4},{4,6},{6,8},{8,10},{10,12},{12,14},{14,0},{1,3},{3,5},... | collective-permute-start | bytes 55304 | tf_op jit(solution)/shard_map/ppermute | solution.py:16
where the time goes:
time: 250 us; the launch traced here: 248 us
  waiting for transfers between devices  114 us (46%)
  starting transfers between devices  51.5 us (21%)
  blocking collectives  35.7 us (14%)
  matrix products  21.8 us (9%)
  local copies, waits for them, and re-layouts  18.2 us (7%)
  other arithmetic  6.43 us (3%)
    psum x1, blocking collectives, body(): kernel_total, skip_total = lax.psum((kernel_part, skip_part), 'seq')  35.7 us
    dot_general x24, matrix products, apply_along(): jnp.einsum('k' + letters[axis_dim] + ',' + letters + '->' + target, matri...  21.8 us
    all_to_all x2, waiting for transfers between devices, sequence_inverse(): lax.all_to_all(pieces, 'seq', split_axis=1, concat_axis=2, tiled=True)  20.5 us
    all_to_all x2, waiting for transfers between devices, sequence_forward(): lax.all_to_all(imaginary, 'seq', split_axis=1, concat_axis=2, tiled=True)  18 us
    all_to_all x2, waiting for transfers between devices, sequence_inverse(): lax.all_to_all(imaginary, 'seq', split_axis=2, concat_axis=1, tiled=True)  17.8 us
    all_to_all x2, waiting for transfers between devices, sequence_forward(): lax.all_to_all(real_part, 'seq', split_axis=1, concat_axis=2, tiled=True)  16.7 us
    all_to_all x2, waiting for transfers between devices, sequence_inverse(): lax.all_to_all(real_part, 'seq', split_axis=2, concat_axis=1, tiled=True)  16.5 us
    all_to_all x2, waiting for transfers between devices, sequence_forward(): lax.all_to_all(signals[:, None], 'seq', split_axis=2, concat_axis=1, tile...  16.4 us
  transfers between devices with their start and end apart: 16, of which 15 were waited for; matrix products, arithmetic and copies ran while one was open for 12% of the time, Pallas kernels for 0%

commit v1 on v0

--- a/solution.py
+++ b/solution.py
@@ -3,6 +3,7 @@
 import jax.numpy as jnp
 from jax import lax
 from jax.sharding import PartitionSpec as P
+from jax.lax import axis_index, axis_size, ppermute
 
 HIGHEST = lax.Precision.HIGHEST
 
@@ -95,11 +96,31 @@
 
 
 def sequence_inverse(real_part, imaginary, extent):
+
+    def matrix_remake(slab_in):
+        lower = axis_size("seq")
+        far_arr = axis_index("seq")
+        arr_next, res = (lower, far_arr)
+        n_now = slab_in.shape[2] // arr_next
+        vec_out = list(slab_in.shape)
+        vec_out[2] = n_now
+        prior = vec_out[1]
+        vec_out[1] = prior * arr_next
+        local_part = jnp.zeros(vec_out, slab_in.dtype)
+        for it in [*range(arr_next)]:
+            u_next = lax.dynamic_slice_in_dim(slab_in, (res ^ it) * n_now, n_now, axis=2)
+            if it:
+                u_next = ppermute(u_next, "seq", [(rr, rr ^ it) for rr in range(arr_next)])
+            local_part = lax.dynamic_update_slice_in_dim(
+                local_part, u_next, (res ^ it) * prior, axis=1
+            )
+        return local_part
+
     devices = lax.axis_size("seq")
     portion = real_part.shape[2] // devices
     real_part, imaginary = inverse_section(real_part, imaginary, 2, True)
     gathered = (
-        lax.all_to_all(real_part, "seq", split_axis=2, concat_axis=1, tiled=True),
+        matrix_remake(real_part),
         lax.all_to_all(imaginary, "seq", split_axis=2, concat_axis=1, tiled=True),
     )
     real_part, imaginary = twist(

time: 250 us -> 238 us (0.952)
  waiting for transfers between devices: 114 us -> 80.2 us
  starting transfers between devices: 51.5 us -> 67.2 us
  local copies, waits for them, and re-layouts: 18.2 us -> 25 us
    ppermute x0 -> x14, starting transfers between devices: none -> 21.4 us  [matrix_remake(): u_next = ppermute(u_next, 'seq', [(rr, rr ^ it) for rr in range(arr_next)])]
    all_to_all x2 -> x0, waiting for transfers between devices: 16.5 us -> none  [sequence_inverse(): lax.all_to_all(real_part, 'seq', split_axis=2, concat_axis=1, tiled=True)]
    all_to_all x2, waiting for transfers between devices: 17.8 us -> 4.07 us  [sequence_inverse(): lax.all_to_all(imaginary, 'seq', split_axis=2, concat_axis=1, tiled=True)]
    all_to_all x2, waiting for transfers between devices: 20.5 us -> 7.86 us  [sequence_inverse(): lax.all_to_all(pieces, 'seq', split_axis=1, concat_axis=2, tiled=True)]
    ppermute x0 -> x14, waiting for transfers between devices: none -> 9.06 us  [matrix_remake(): u_next = ppermute(u_next, 'seq', [(rr, rr ^ it) for rr in range(arr_next)])]
    all_to_all x2 -> x0, starting transfers between devices: 7.73 us -> none  [sequence_inverse(): lax.all_to_all(real_part, 'seq', split_axis=2, concat_axis=1, tiled=True)]
    dynamic_update_slice x0 -> x16, local copies, waits for them, and re-layouts: none -> 6.28 us  [matrix_remake(): lax.dynamic_update_slice_in_dim(local_part, u_next, (res ^ it) * prior, a...]
    sub x2 -> x0, local copies, waits for them, and re-layouts: 2.87 us -> none  [inverse_section(): apply_along(cosine, real_part, axis_dim)]
  transfers between devices with their start and end apart: 16 -> 28, of which waited for: 15 -> 15; matrix products, arithmetic and copies ran while one was open for 12% -> 14% of each run, Pallas kernels for 0% -> 0%
where the time goes in v1:
time: 238 us; the launch traced here: 237 us
  waiting for transfers between devices  80.2 us (34%)
  starting transfers between devices  67.2 us (28%)
  blocking collectives  34.9 us (15%)
  local copies, waits for them, and re-layouts  25 us (11%)
  matrix products  21.6 us (9%)
  other arithmetic  6.3 us (3%)
    psum x1, blocking collectives, body(): kernel_total, skip_total = lax.psum((kernel_part, skip_part), 'seq')  34.9 us
    dot_general x24, matrix products, apply_along(): jnp.einsum('k' + letters[axis_dim] + ',' + letters + '->' + target, matri...  21.6 us
    ppermute x14, starting transfers between devices, matrix_remake(): u_next = ppermute(u_next, 'seq', [(rr, rr ^ it) for rr in range(arr_next)])  21.4 us
    all_to_all x2, waiting for transfers between devices, sequence_forward(): lax.all_to_all(imaginary, 'seq', split_axis=1, concat_axis=2, tiled=True)  18 us
    all_to_all x2, waiting for transfers between devices, sequence_forward(): lax.all_to_all(real_part, 'seq', split_axis=1, concat_axis=2, tiled=True)  16.6 us
    all_to_all x2, waiting for transfers between devices, sequence_forward(): lax.all_to_all(signals[:, None], 'seq', split_axis=2, concat_axis=1, tile...  16.4 us
    all_to_all x2, starting transfers between devices, sequence_inverse(): lax.all_to_all(imaginary, 'seq', split_axis=2, concat_axis=1, tiled=True)  9.34 us
    ppermute x14, waiting for transfers between devices, matrix_remake(): u_next = ppermute(u_next, 'seq', [(rr, rr ^ it) for rr in range(arr_next)])  9.06 us
  transfers between devices with their start and end apart: 28, of which 15 were waited for; matrix products, arithmetic and copies ran while one was open for 14% of the time, Pallas kernels for 0%

profile of v1, /device:TPU:0, one launch (start us, length us, event | category | flops | bytes accessed | tf_op | source)
XLA Modules:
  0.0 236.7 jit_solution(6122357659631129663)
XLA Ops:
  1.4 6.0 %collective-permute-start.1 = (bf16[3,3,512]{2,1,0:T(4,128)(2,1)S(1)}, bf16[3,3,512]{2,1,0:T(4,128)(2,1)S(1)}, u32[]{:S(2)}, u32[]{:S(2)}) collective-permute-start(bf16[3,3,512]{2,1,0:T(4,128)(2,1)S(1)} %get-tuple-element.58), channel_id=1, source_target_pairs={{2,0},{4,2},{6,4},{8,6},{10,8},{12,10},{14,12},{0,14},{3,1},{5,3},... | collective-permute-start | bytes 27656 | tf_op jit(solution)/shard_map/ppermute | solution.py:20
  8.9 5.0 %collective-permute-done = bf16[3,3,512]{2,1,0:T(4,128)(2,1)S(1)} collective-permute-done((bf16[3,3,512]{2,1,0:T(4,128)(2,1)S(1)}, bf16[3,3,512]{2,1,0:T(4,128)(2,1)S(1)}, u32[]{:S(2)}, u32[]{:S(2)}) %collective-permute-start) | collective-permute-done | bytes 9248 | tf_op jit(solution)/shard_map/ppermute | solution.py:17
  15.8 3.4 %all-to-all-start.5 = ((f32[1,1,128,512]{3,1,0,2:T(1,128)}), f32[1,1,128,512]{3,1,0,2:T(1,128)S(1)}, u32[]{:S(2)}, u32[]{:S(2)}) async-start(f32[1,1,128,512]{3,1,0,2:T(1,128)} %copy.54), calls=%async_computation.5 | async-start | bytes 524288 | tf_op jit(solution)/shard_map/all_to_all | solution.py:88
  21.4 6.0 %all-to-all-done.5 = f32[1,1,128,512]{3,1,0,2:T(1,128)S(1)} async-done(((f32[1,1,128,512]{3,1,0,2:T(1,128)}), f32[1,1,128,512]{3,1,0,2:T(1,128)S(1)}, u32[]{:S(2)}, u32[]{:S(2)}) %all-to-all-start.5) | async-done | bytes 262176 | tf_op jit(solution)/shard_map/all_to_all | solution.py:88
  27.3 3.5 %all-to-all-start = ((f32[2,1,128,512]{3,0,1,2:T(2,128)}), f32[2,1,128,512]{3,0,1,2:T(2,128)S(1)}, u32[]{:S(2)}, u32[]{:S(2)}) async-start(f32[2,1,128,512]{3,0,1,2:T(2,128)} %copy.38), calls=%async_computation | async-start | bytes 1048576 | tf_op jit(solution)/shard_map/all_to_all | solution.py:88
  33.0 10.4 %all-to-all-done = f32[2,1,128,512]{3,0,1,2:T(2,128)S(1)} async-done(((f32[2,1,128,512]{3,0,1,2:T(2,128)}), f32[2,1,128,512]{3,0,1,2:T(2,128)S(1)}, u32[]{:S(2)}, u32[]{:S(2)}) %all-to-all-start) | async-done | bytes 524320 | tf_op jit(solution)/shard_map/all_to_all | solution.py:88
  43.4 3.6 %all-to-all-start.6 = ((f32[1,8,16,512]{3,2,0,1:T(8,128)}), f32[1,8,16,512]{3,2,0,1:T(8,128)S(1)}, u32[]{:S(2)}, u32[]{:S(2)}) async-start(f32[1,8,16,512]{3,2,0,1:T(8,128)} %copy.57), calls=%async_computation.6 | async-start | bytes 524288 | tf_op jit(solution)/shard_map/all_to_all | solution.py:92
  48.0 7.3 %all-to-all-done.6 = f32[1,8,16,512]{3,2,0,1:T(8,128)S(1)} async-done(((f32[1,8,16,512]{3,2,0,1:T(8,128)}), f32[1,8,16,512]{3,2,0,1:T(8,128)S(1)}, u32[]{:S(2)}, u32[]{:S(2)}) %all-to-all-start.6) | async-done | bytes 262176 | tf_op jit(solution)/shard_map/all_to_all | solution.py:92
  55.3 3.4 %all-to-all-start.7 = ((f32[1,8,16,512]{3,2,0,1:T(8,128)}), f32[1,8,16,512]{3,2,0,1:T(8,128)S(1)}, u32[]{:S(2)}, u32[]{:S(2)}) async-start(f32[1,8,16,512]{3,2,0,1:T(8,128)} %copy.58), calls=%async_computation.7 | async-start | bytes 524288 | tf_op jit(solution)/shard_map/all_to_all | solution.py:93
  61.7 5.2 %all-to-all-done.7 = f32[1,8,16,512]{3,2,0,1:T(8,128)S(1)} async-done(((f32[1,8,16,512]{3,2,0,1:T(8,128)}), f32[1,8,16,512]{3,2,0,1:T(8,128)S(1)}, u32[]{:S(2)}, u32[]{:S(2)}) %all-to-all-start.7) | async-done | bytes 262176 | tf_op jit(solution)/shard_map/all_to_all | solution.py:93
  66.9 3.5 %all-to-all-start.2 = ((f32[2,8,16,512]{3,2,0,1:T(8,128)}), f32[2,8,16,512]{3,2,0,1:T(8,128)S(1)}, u32[]{:S(2)}, u32[]{:S(2)}) async-start(f32[2,8,16,512]{3,2,0,1:T(8,128)} %copy.45), calls=%async_computation.2 | async-start | bytes 1048576 | tf_op jit(solution)/shard_map/all_to_all | solution.py:93
  71.5 12.8 %all-to-all-done.2 = f32[2,8,16,512]{3,2,0,1:T(8,128)S(1)} async-done(((f32[2,8,16,512]{3,2,0,1:T(8,128)}), f32[2,8,16,512]{3,2,0,1:T(8,128)S(1)}, u32[]{:S(2)}, u32[]{:S(2)}) %all-to-all-start.2) | async-done | bytes 524320 | tf_op jit(solution)/shard_map/all_to_all | solution.py:93
  84.3 3.7 %all-to-all-start.1 = ((f32[2,8,16,512]{3,2,0,1:T(8,128)}), f32[2,8,16,512]{3,2,0,1:T(8,128)S(1)}, u32[]{:S(2)}, u32[]{:S(2)}) async-start(f32[2,8,16,512]{3,2,0,1:T(8,128)} %copy.42), calls=%async_computation.1 | async-start | bytes 1048576 | tf_op jit(solution)/shard_map/all_to_all | solution.py:92
  92.8 9.3 %all-to-all-done.1 = f32[2,8,16,512]{3,2,0,1:T(8,128)S(1)} async-done(((f32[2,8,16,512]{3,2,0,1:T(8,128)}), f32[2,8,16,512]{3,2,0,1:T(8,128)S(1)}, u32[]{:S(2)}, u32[]{:S(2)}) %all-to-all-start.1) | async-done | bytes 524320 | tf_op jit(solution)/shard_map/all_to_all | solution.py:92
  113.1 4.4 %all-to-all-start.8 = ((f32[2,1,128,512]{3,0,1,2:T(2,128)}), f32[2,1,128,512]{3,0,1,2:T(2,128)}, u32[]{:S(2)}, u32[]{:S(2)}) async-start(f32[2,1,128,512]{3,0,1,2:T(2,128)} %copy.61), calls=%async_computation.8 | async-start | bytes 1048576 | tf_op jit(solution)/shard_map/all_to_all | solution.py:124
  131.2 3.4 %collective-permute-start.14 = (f32[2,1,16,512]{3,1,2,0:T(1,128)S(1)}, f32[2,1,16,512]{3,1,2,0:T(1,128)S(1)}, u32[]{:S(2)}, u32[]{:S(2)}) collective-permute-start(f32[2,1,16,512]{3,1,2,0:T(1,128)S(1)} %reshape_bitcast_fusion.1), channel_id=1, source_target_pairs={{0,12},{2,14},{4,8},{6,10},{8,4},{10,6},{12,0},{14,2},{1,13},{3,15... | collective-permute-start | bytes 196616 | tf_op jit(solution)/shard_map/ppermute | solution.py:113
  144.0 5.0 %all-to-all-start.3 = ((f32[1,1,128,512]{3,1,0,2:T(1,128)}), f32[1,1,128,512]{3,1,0,2:T(1,128)S(1)}, u32[]{:S(2)}, u32[]{:S(2)}) async-start(f32[1,1,128,512]{3,1,0,2:T(1,128)} %copy.50), calls=%async_computation.3 | async-start | bytes 524288 | tf_op jit(solution)/shard_map/all_to_all | solution.py:124
  153.1 4.1 %all-to-all-done.3 = f32[1,1,128,512]{3,1,0,2:T(1,128)S(1)} async-done(((f32[1,1,128,512]{3,1,0,2:T(1,128)}), f32[1,1,128,512]{3,1,0,2:T(1,128)S(1)}, u32[]{:S(2)}, u32[]{:S(2)}) %all-to-all-start.3) | async-done | bytes 262176 | tf_op jit(solution)/shard_map/all_to_all | solution.py:124
  157.2 3.5 %all-to-all-start.9 = ((f32[2,8,16,512]{3,2,0,1:T(8,128)}), f32[2,8,16,512]{3,2,0,1:T(8,128)S(1)}, u32[]{:S(2)}, u32[]{:S(2)}) async-start(f32[2,8,16,512]{3,2,0,1:T(8,128)} %copy.65), calls=%async_computation.9 | async-start | bytes 1048576 | tf_op jit(solution)/shard_map/all_to_all | solution.py:130
  165.2 3.4 %collective-permute-start.7 = (f32[1,1,16,512]{3,1,2,0:T(1,128)S(1)}, f32[1,1,16,512]{3,1,2,0:T(1,128)S(1)}, u32[]{:S(2)}, u32[]{:S(2)}) collective-permute-start(f32[1,1,16,512]{3,1,2,0:T(1,128)S(1)} %reshape_bitcast_fusion.9), channel_id=1, source_target_pairs={{0,12},{2,14},{4,8},{6,10},{8,4},{10,6},{12,0},{14,2},{1,13},{3,15... | collective-permute-start | bytes 98312 | tf_op jit(solution)/shard_map/ppermute | solution.py:113
  169.4 5.8 %collective-permute-done.5 = f32[1,1,16,512]{3,1,2,0:T(1,128)S(1)} collective-permute-done((f32[1,1,16,512]{3,1,2,0:T(1,128)S(1)}, f32[1,1,16,512]{3,1,2,0:T(1,128)S(1)}, u32[]{:S(2)}, u32[]{:S(2)}) %collective-permute-start.5) | collective-permute-done | bytes 32800 | tf_op jit(solution)/shard_map/ppermute | solution.py:113
  178.9 3.7 %all-to-all-start.4 = ((f32[1,8,16,512]{3,2,0,1:T(8,128)}), f32[1,8,16,512]{3,2,0,1:T(8,128)S(1)}, u32[]{:S(2)}, u32[]{:S(2)}) async-start(f32[1,8,16,512]{3,2,0,1:T(8,128)} %copy.53), calls=%async_computation.4 | async-start | bytes 524288 | tf_op jit(solution)/shard_map/all_to_all | solution.py:130
  182.6 7.9 %all-to-all-done.4 = f32[1,8,16,512]{3,2,0,1:T(8,128)S(1)} async-done(((f32[1,8,16,512]{3,2,0,1:T(8,128)}), f32[1,8,16,512]{3,2,0,1:T(8,128)S(1)}, u32[]{:S(2)}, u32[]{:S(2)}) %all-to-all-start.4) | async-done | bytes 262176 | tf_op jit(solution)/shard_map/all_to_all | solution.py:130
  193.1 34.9 %all-reduce = (f32[3,7,512]{2,0,1:T(4,128)S(1)}, f32[512]{0:T(512)S(1)}) all-reduce(f32[3,7,512]{2,0,1:T(4,128)S(1)} %constant_dynamic-update-slice_fusion.2, f32[512]{0:T(512)S(1)} %get-tuple-element.38), channel_id=1, replica_groups=mesh['groups'=2,'seq'=8,'chan'=2] {'seq'}, use_global_device_ids=true, to_apply=%region_7.8 | all-reduce | flops 11264 | bytes 90112 | tf_op jit(solution)/shard_map/psum | solution.py:192
  (154 shorter events, 76.2 us)
Async XLA Ops:
  15.8 11.6 %all-to-all-start.5 = ((f32[1,1,128,512]{3,1,0,2:T(1,128)}), f32[1,1,128,512]{3,1,0,2:T(1,128)S(1)}, u32[]{:S(2)}, u32[]{:S(2)}) async-start(f32[1,1,128,512]{3,1,0,2:T(1,128)} %copy.54), calls=%async_computation.5 | async-start | bytes 524288 | tf_op jit(solution)/shard_map/all_to_all | solution.py:88
  27.3 16.0 %all-to-all-start = ((f32[2,1,128,512]{3,0,1,2:T(2,128)}), f32[2,1,128,512]{3,0,1,2:T(2,128)S(1)}, u32[]{:S(2)}, u32[]{:S(2)}) async-start(f32[2,1,128,512]{3,0,1,2:T(2,128)} %copy.38), calls=%async_computation | async-start | bytes 1048576 | tf_op jit(solution)/shard_map/all_to_all | solution.py:88
  43.4 11.9 %all-to-all-start.6 = ((f32[1,8,16,512]{3,2,0,1:T(8,128)}), f32[1,8,16,512]{3,2,0,1:T(8,128)S(1)}, u32[]{:S(2)}, u32[]{:S(2)}) async-start(f32[1,8,16,512]{3,2,0,1:T(8,128)} %copy.57), calls=%async_computation.6 | async-start | bytes 524288 | tf_op jit(solution)/shard_map/all_to_all | solution.py:92
  55.3 11.6 %all-to-all-start.7 = ((f32[1,8,16,512]{3,2,0,1:T(8,128)}), f32[1,8,16,512]{3,2,0,1:T(8,128)S(1)}, u32[]{:S(2)}, u32[]{:S(2)}) async-start(f32[1,8,16,512]{3,2,0,1:T(8,128)} %copy.58), calls=%async_computation.7 | async-start | bytes 524288 | tf_op jit(solution)/shard_map/all_to_all | solution.py:93
  66.9 17.4 %all-to-all-start.2 = ((f32[2,8,16,512]{3,2,0,1:T(8,128)}), f32[2,8,16,512]{3,2,0,1:T(8,128)S(1)}, u32[]{:S(2)}, u32[]{:S(2)}) async-start(f32[2,8,16,512]{3,2,0,1:T(8,128)} %copy.45), calls=%async_computation.2 | async-start | bytes 1048576 | tf_op jit(solution)/shard_map/all_to_all | solution.py:93
  84.3 17.9 %all-to-all-start.1 = ((f32[2,8,16,512]{3,2,0,1:T(8,128)}), f32[2,8,16,512]{3,2,0,1:T(8,128)S(1)}, u32[]{:S(2)}, u32[]{:S(2)}) async-start(f32[2,8,16,512]{3,2,0,1:T(8,128)} %copy.42), calls=%async_computation.1 | async-start | bytes 1048576 | tf_op jit(solution)/shard_map/all_to_all | solution.py:92
  113.1 30.9 %all-to-all-start.8 = ((f32[2,1,128,512]{3,0,1,2:T(2,128)}), f32[2,1,128,512]{3,0,1,2:T(2,128)}, u32[]{:S(2)}, u32[]{:S(2)}) async-start(f32[2,1,128,512]{3,0,1,2:T(2,128)} %copy.61), calls=%async_computation.8 | async-start | bytes 1048576 | tf_op jit(solution)/shard_map/all_to_all | solution.py:124
  119.2 12.0 %collective-permute-start.9 = (f32[2,1,16,512]{3,1,2,0:T(1,128)}, f32[2,1,16,512]{3,1,2,0:T(1,128)S(1)}, u32[]{:S(2)}, u32[]{:S(2)}) collective-permute-start(f32[2,1,16,512]{3,1,2,0:T(1,128)} %reshape_bitcast_fusion.6), channel_id=1, source_target_pairs={{0,2},{2,0},{4,6},{6,4},{8,10},{10,8},{12,14},{14,12},{1,3},{3,1},... | collective-permute-start | bytes 196616 | tf_op jit(solution)/shard_map/ppermute | solution.py:113
  121.5 13.1 %collective-permute-start.10 = (f32[2,1,16,512]{3,1,2,0:T(1,128)}, f32[2,1,16,512]{3,1,2,0:T(1,128)}, u32[]{:S(2)}, u32[]{:S(2)}) collective-permute-start(f32[2,1,16,512]{3,1,2,0:T(1,128)} %reshape_bitcast_fusion.5), channel_id=1, source_target_pairs={{0,4},{2,6},{4,0},{6,2},{8,12},{10,14},{12,8},{14,10},{1,5},{3,7},... | collective-permute-start | bytes 196616 | tf_op jit(solution)/shard_map/ppermute | solution.py:113
  123.7 13.1 %collective-permute-start.11 = (f32[2,1,16,512]{3,1,2,0:T(1,128)}, f32[2,1,16,512]{3,1,2,0:T(1,128)S(1)}, u32[]{:S(2)}, u32[]{:S(2)}) collective-permute-start(f32[2,1,16,512]{3,1,2,0:T(1,128)} %reshape_bitcast_fusion.4), channel_id=1, source_target_pairs={{0,6},{2,4},{4,2},{6,0},{8,14},{10,12},{12,10},{14,8},{1,7},{3,5},... | collective-permute-start | bytes 196616 | tf_op jit(solution)/shard_map/ppermute | solution.py:113
  124.1 15.3 %collective-permute-start.12 = (f32[2,1,16,512]{3,1,2,0:T(1,128)S(1)}, f32[2,1,16,512]{3,1,2,0:T(1,128)S(1)}, u32[]{:S(2)}, u32[]{:S(2)}) collective-permute-start(f32[2,1,16,512]{3,1,2,0:T(1,128)S(1)} %reshape_bitcast_fusion.3), channel_id=1, source_target_pairs={{0,8},{2,10},{4,12},{6,14},{8,0},{10,2},{12,4},{14,6},{1,9},{3,11}... | collective-permute-start | bytes 196616 | tf_op jit(solution)/shard_map/ppermute | solution.py:113
  126.8 15.0 %collective-permute-start.13 = (f32[2,1,16,512]{3,1,2,0:T(1,128)S(1)}, f32[2,1,16,512]{3,1,2,0:T(1,128)S(1)}, u32[]{:S(2)}, u32[]{:S(2)}) collective-permute-start(f32[2,1,16,512]{3,1,2,0:T(1,128)S(1)} %reshape_bitcast_fusion.2), channel_id=1, source_target_pairs={{0,10},{2,8},{4,14},{6,12},{8,2},{10,0},{12,6},{14,4},{1,11},{3,9}... | collective-permute-start | bytes 196616 | tf_op jit(solution)/shard_map/ppermute | solution.py:113
  131.2 11.6 %collective-permute-start.14 = (f32[2,1,16,512]{3,1,2,0:T(1,128)S(1)}, f32[2,1,16,512]{3,1,2,0:T(1,128)S(1)}, u32[]{:S(2)}, u32[]{:S(2)}) collective-permute-start(f32[2,1,16,512]{3,1,2,0:T(1,128)S(1)} %reshape_bitcast_fusion.1), channel_id=1, source_target_pairs={{0,12},{2,14},{4,8},{6,10},{8,4},{10,6},{12,0},{14,2},{1,13},{3,15... | collective-permute-start | bytes 196616 | tf_op jit(solution)/shard_map/ppermute | solution.py:113
  134.6 8.8 %collective-permute-start.15 = (f32[2,1,16,512]{3,1,2,0:T(1,128)S(1)}, f32[2,1,16,512]{3,1,2,0:T(1,128)S(1)}, u32[]{:S(2)}, u32[]{:S(2)}) collective-permute-start(f32[2,1,16,512]{3,1,2,0:T(1,128)S(1)} %reshape_bitcast_fusion), channel_id=1, source_target_pairs={{0,14},{2,12},{4,10},{6,8},{8,6},{10,4},{12,2},{14,0},{1,15},{3,13... | collective-permute-start | bytes 196616 | tf_op jit(solution)/shard_map/ppermute | solution.py:113
  136.8 28.4 %collective-permute-start.2 = (f32[1,1,16,512]{3,1,2,0:T(1,128)S(1)}, f32[1,1,16,512]{3,1,2,0:T(1,128)S(1)}, u32[]{:S(2)}, u32[]{:S(2)}) collective-permute-start(f32[1,1,16,512]{3,1,2,0:T(1,128)S(1)} %reshape_bitcast_fusion.14), channel_id=1, source_target_pairs={{0,2},{2,0},{4,6},{6,4},{8,10},{10,8},{12,14},{14,12},{1,3},{3,1},... | collective-permute-start | bytes 98312 | tf_op jit(solution)/shard_map/ppermute | solution.py:113
  139.3 29.3 %collective-permute-start.3 = (f32[1,1,16,512]{3,1,2,0:T(1,128)S(1)}, f32[1,1,16,512]{3,1,2,0:T(1,128)S(1)}, u32[]{:S(2)}, u32[]{:S(2)}) collective-permute-start(f32[1,1,16,512]{3,1,2,0:T(1,128)S(1)} %reshape_bitcast_fusion.13), channel_id=1, source_target_pairs={{0,4},{2,6},{4,0},{6,2},{8,12},{10,14},{12,8},{14,10},{1,5},{3,7},... | collective-permute-start | bytes 98312 | tf_op jit(solution)/shard_map/ppermute | solution.py:113
  141.8 27.4 %collective-permute-start.4 = (f32[1,1,16,512]{3,1,2,0:T(1,128)S(1)}, f32[1,1,16,512]{3,1,2,0:T(1,128)S(1)}, u32[]{:S(2)}, u32[]{:S(2)}) collective-permute-start(f32[1,1,16,512]{3,1,2,0:T(1,128)S(1)} %reshape_bitcast_fusion.12), channel_id=1, source_target_pairs={{0,6},{2,4},{4,2},{6,0},{8,14},{10,12},{12,10},{14,8},{1,7},{3,5},... | collective-permute-start | bytes 98312 | tf_op jit(solution)/shard_map/ppermute | solution.py:113
  144.0 13.2 %all-to-all-start.3 = ((f32[1,1,128,512]{3,1,0,2:T(1,128)}), f32[1,1,128,512]{3,1,0,2:T(1,128)S(1)}, u32[]{:S(2)}, u32[]{:S(2)}) async-start(f32[1,1,128,512]{3,1,0,2:T(1,128)} %copy.50), calls=%async_computation.3 | async-start | bytes 524288 | tf_op jit(solution)/shard_map/all_to_all | solution.py:124
  157.2 21.7 %all-to-all-start.9 = ((f32[2,8,16,512]{3,2,0,1:T(8,128)}), f32[2,8,16,512]{3,2,0,1:T(8,128)S(1)}, u32[]{:S(2)}, u32[]{:S(2)}) async-start(f32[2,8,16,512]{3,2,0,1:T(8,128)} %copy.65), calls=%async_computation.9 | async-start | bytes 1048576 | tf_op jit(solution)/shard_map/all_to_all | solution.py:130
  160.7 14.4 %collective-permute-start.5 = (f32[1,1,16,512]{3,1,2,0:T(1,128)S(1)}, f32[1,1,16,512]{3,1,2,0:T(1,128)S(1)}, u32[]{:S(2)}, u32[]{:S(2)}) collective-permute-start(f32[1,1,16,512]{3,1,2,0:T(1,128)S(1)} %reshape_bitcast_fusion.11), channel_id=1, source_target_pairs={{0,8},{2,10},{4,12},{6,14},{8,0},{10,2},{12,4},{14,6},{1,9},{3,11}... | collective-permute-start | bytes 98312 | tf_op jit(solution)/shard_map/ppermute | solution.py:113
  163.7 12.7 %collective-permute-start.6 = (f32[1,1,16,512]{3,1,2,0:T(1,128)S(1)}, f32[1,1,16,512]{3,1,2,0:T(1,128)S(1)}, u32[]{:S(2)}, u32[]{:S(2)}) collective-permute-start(f32[1,1,16,512]{3,1,2,0:T(1,128)S(1)} %reshape_bitcast_fusion.10), channel_id=1, source_target_pairs={{0,10},{2,8},{4,14},{6,12},{8,2},{10,0},{12,6},{14,4},{1,11},{3,9}... | collective-permute-start | bytes 98312 | tf_op jit(solution)/shard_map/ppermute | solution.py:113
  165.2 11.3 %collective-permute-start.7 = (f32[1,1,16,512]{3,1,2,0:T(1,128)S(1)}, f32[1,1,16,512]{3,1,2,0:T(1,128)S(1)}, u32[]{:S(2)}, u32[]{:S(2)}) collective-permute-start(f32[1,1,16,512]{3,1,2,0:T(1,128)S(1)} %reshape_bitcast_fusion.9), channel_id=1, source_target_pairs={{0,12},{2,14},{4,8},{6,10},{8,4},{10,6},{12,0},{14,2},{1,13},{3,15... | collective-permute-start | bytes 98312 | tf_op jit(solution)/shard_map/ppermute | solution.py:113
  168.6 8.1 %collective-permute-start.8 = (f32[1,1,16,512]{3,1,2,0:T(1,128)S(1)}, f32[1,1,16,512]{3,1,2,0:T(1,128)S(1)}, u32[]{:S(2)}, u32[]{:S(2)}) collective-permute-start(f32[1,1,16,512]{3,1,2,0:T(1,128)S(1)} %reshape_bitcast_fusion.8), channel_id=1, source_target_pairs={{0,14},{2,12},{4,10},{6,8},{8,6},{10,4},{12,2},{14,0},{1,15},{3,13... | collective-permute-start | bytes 98312 | tf_op jit(solution)/shard_map/ppermute | solution.py:113
  178.9 11.6 %all-to-all-start.4 = ((f32[1,8,16,512]{3,2,0,1:T(8,128)}), f32[1,8,16,512]{3,2,0,1:T(8,128)S(1)}, u32[]{:S(2)}, u32[]{:S(2)}) async-start(f32[1,8,16,512]{3,2,0,1:T(8,128)} %copy.53), calls=%async_computation.4 | async-start | bytes 524288 | tf_op jit(solution)/shard_map/all_to_all | solution.py:130
  (11 other events, 49.6 us)
